TPU v7x, 512 devices: a whole 4x4x16 slice. The times are simulated.
512 devices in a mesh: group: 16 (over y, z_hi), seq: 32 (over x, z_lo, core).
Axes of the slice: x: 4, y: 4, z: 16 (z_hi: 4, z_lo: 4; z = z_hi * 4 + z_lo), core: 2. Of those that a mesh axis runs over, the one named last changes fastest.
Arguments:
- features: bfloat16 [65536, 768], P(('group', 'seq')), may hold values from -6 to 6
- tiles: bfloat16 [65536, 1024], P(('group', 'seq')), may hold values from -0.5 to 0.5
- tile_src: int32 [512, 8], P(('group', 'seq')), may hold values from 0 to 15
- tile_count: int32 [512], P(('group', 'seq')), may hold values from 1 to 8, as said below
- node_bucket: int32 [65536], P(('group', 'seq')), may hold values from 0 to 15
- w_qk: bfloat16 [768, 1536], replicated, may hold values from -0.3125 to 0.3125
- w_v: bfloat16 [768, 768], replicated, may hold values from -1.25 to 1.25
- bias_table: float32 [32, 256], replicated, may hold values from -2 to 300
Outputs:
- attended: bfloat16 [65536, 768], P(('group', 'seq'))
Inputs may be any that keep to these rules, and one draw needn't show every extreme that they name: `tile_count`: some row block uses all 8 slots.
All inputs are finite; a program needn't handle non-finite values.
Results may differ from a plain program's by a relative error of at most 0.012.
Values may be sent and summed in bfloat16 or wider, within the bound.
A program may use at most 64 MiB of HBM per device.

v0:
```python
import math

import jax
import jax.numpy as jnp
from jax import lax
from jax.sharding import PartitionSpec as P

H = 32
HD = 24
NB = 16
TILES = 8


def on_device(features, tiles, tile_src, tile_count, node_bucket, w_qk, w_v, bias_table):
    row_count, feat_width = features.shape
    group_count = lax.axis_size("group")
    live_flag = jnp.arange(TILES) < tile_count[0]
    tile_rows = tiles.reshape(row_count, TILES, row_count)
    sources = tile_src[0]
    gathered = lax.all_gather(features, "group", axis=0, tiled=True)
    chosen = gathered.reshape(group_count, row_count, feat_width)[sources]
    masked = tile_rows * live_flag.astype(jnp.bfloat16)[None, :, None]
    aggregated = features.astype(jnp.float32) + jnp.einsum(
        "rtc,tcd->rd", masked, chosen, preferred_element_type=jnp.float32
    )
    mean_square = jnp.mean(aggregated * aggregated, axis=-1, keepdims=True)
    normed = (aggregated * lax.rsqrt(mean_square + 1e-06)).astype(jnp.bfloat16)
    query_key = jnp.dot(normed, w_qk, preferred_element_type=jnp.float32).astype(jnp.bfloat16)
    values = jnp.dot(normed, w_v, preferred_element_type=jnp.float32).astype(jnp.bfloat16)
    bias_cube = bias_table.reshape(H, NB, NB)
    scale = 1.0 / math.sqrt(HD)
    iota_nb = jnp.arange(NB)
    queries = query_key[:, :feat_width].reshape(row_count, H, HD)
    keys_own = query_key[:, feat_width:]
    query_bias = bias_cube[:, node_bucket, :]
    start_state = (
        jnp.full((H, row_count), -1e30, jnp.float32),
        jnp.zeros((H, row_count), jnp.float32),
        jnp.zeros((H, row_count, HD), jnp.float32),
    )
    key_rows = lax.all_gather(keys_own, "seq", axis=0, tiled=True)
    value_rows = lax.all_gather(values, "seq", axis=0, tiled=True)
    bucket_rows = lax.all_gather(node_bucket, "seq", axis=0, tiled=True)
    key_total = key_rows.shape[0]
    key_block = math.gcd(key_total, 512)

    def one_block(block_index, state_in):
        peak_old, total_old, accum_old = state_in
        offset = block_index * key_block
        key_part = lax.dynamic_slice_in_dim(key_rows, offset, key_block, 0).reshape(
            key_block, H, HD
        )
        value_part = lax.dynamic_slice_in_dim(value_rows, offset, key_block, 0).reshape(
            key_block, H, HD
        )
        bucket_part = lax.dynamic_slice_in_dim(bucket_rows, offset, key_block, 0)
        onehot = (bucket_part[:, None] == iota_nb[None, :]).astype(jnp.float32)
        scores = (
            jnp.einsum("rhd,nhd->hrn", queries, key_part, preferred_element_type=jnp.float32)
            * scale
        )
        scores = scores + jnp.einsum(
            "hrb,nb->hrn", query_bias, onehot, precision=lax.Precision.HIGHEST
        )
        peak_new = jnp.maximum(peak_old, jnp.max(scores, axis=-1))
        factor = jnp.exp(peak_old - peak_new)
        weights = jnp.exp(scores - peak_new[..., None])
        total_new = total_old * factor + jnp.sum(weights, axis=-1)
        accum_new = accum_old * factor[..., None] + jnp.einsum(
            "hrn,nhd->hrd",
            weights.astype(jnp.bfloat16),
            value_part,
            preferred_element_type=jnp.float32,
        )
        return (peak_new, total_new, accum_new)

    peak_end, total_end, accum_end = lax.fori_loop(
        0, key_total // key_block, one_block, start_state
    )
    heads_out = accum_end / total_end[..., None]
    attended = heads_out.transpose(1, 0, 2).reshape(row_count, feat_width).astype(jnp.bfloat16)
    return attended


def solution(mesh):
    in_specs = (
        P(("group", "seq"), None),
        P(("group", "seq"), None),
        P(("group", "seq"), None),
        P(("group", "seq")),
        P(("group", "seq")),
        P(),
        P(),
        P(),
    )
    out_specs = P(("group", "seq"), None)
    return jax.shard_map(
        on_device, mesh=mesh, in_specs=in_specs, out_specs=out_specs, check_vma=False
    )
```

profile of v0, /device:TPU:1, one launch (start us, length us, event | category | flops | bytes accessed | tf_op | source)
XLA Modules:
  0.0 412.8 jit_solution(12334973029780764622)
XLA Ops:
  8.6 121.5 %all-gather.5.cloned.1.call-done = bf16[2048,768]{1,0:T(8,128)(2,1)} async-done(((bf16[128,768]{1,0:T(8,128)(2,1)}), bf16[2048,768]{1,0:T(8,128)(2,1)}) %all-gather.5.cloned.1.call-update) | async-done | bytes 3145744 | tf_op jit(solution)/shard_map/all_gather | solution.py:20
  130.1 3.7 gather_fusion
  137.1 2.3 convolution_convert_fusion.1
  141.4 2.4 copy.28
  143.7 39.3 %all-gather = s32[32,1,128]{2,1,0:T(1,128)S(1)} all-gather(s32[1,1,128]{2,1,0:T(1,128)S(1)} %bitcast.66), channel_id=1, replica_groups=mesh['group'=16,'seq'=32] {'seq'}, dimensions={0}, use_global_device_ids=true | all-gather | bytes 16896 | tf_op jit(solution)/shard_map/all_gather | solution.py:43
  183.9 19.7 %all-gather.7.cloned.1.call-done = bf16[4096,768]{1,0:T(8,128)(2,1)} async-done(((bf16[128,768]{1,0:T(8,128)(2,1)}), bf16[4096,768]{1,0:T(8,128)(2,1)}) %all-gather.7.cloned.1.call-update) | async-done | bytes 6291472 | tf_op jit(solution)/shard_map/all_gather | solution.py:41
  203.6 71.9 %all-gather.9.cloned.1.call-done = bf16[4096,768]{1,0:T(8,128)(2,1)} async-done(((bf16[128,768]{1,0:T(8,128)(2,1)}), bf16[4096,768]{1,0:T(8,128)(2,1)}) %all-gather.9.cloned.1.call-update) | async-done | bytes 6291472 | tf_op jit(solution)/shard_map/all_gather | solution.py:42
  275.5 129.1 %while.18 = (s32[]{:T(128)}, f32[32,128]{1,0:T(8,128)S(1)}, f32[32,128]{1,0:T(8,128)}, f32[32,128,24]{1,2,0:T(8,128)S(1)}, bf16[4096,768]{1,0:T(8,128)(2,1)}, /*...) while((s32[]{:T(128)}, f32[32,128]{1,0:T(8,128)S(1)}, ...), condition=%wide.region_4.0_spmd.clone, body=%wide.region_1.0_spmd.clone.sunk | while | flops 618983424 | bytes 55515500 | solution.py:77
  276.2 2.7 constant_dynamic-slice_fusion.3
  280.3 2.4 copy.44
  282.7 4.5 %fusion.46 = f32[512,32,128]{2,0,1:T(8,128)S(1)} fusion(f32[32,128,16]{1,2,0:T(8,128)} %get-tuple-element.364, s32[512]{0:T(512)} %dynamic_slice.29), kind=kOutput, calls=%fused_computation.13.clone.1 | convolution fusion | flops 402661376 | bytes 8652800 | tf_op jit(solution)/shard_map/while/body/eval_jaxpr/hrb,nb->hrn/dot_general | solution.py:62
  292.4 2.7 constant_dynamic-slice_fusion.3
  296.4 2.4 copy.44
  298.8 4.5 %fusion.46 = f32[512,32,128]{2,0,1:T(8,128)S(1)} fusion(f32[32,128,16]{1,2,0:T(8,128)} %get-tuple-element.364, s32[512]{0:T(512)} %dynamic_slice.29), kind=kOutput, calls=%fused_computation.13.clone.1 | convolution fusion | flops 402661376 | bytes 8652800 | tf_op jit(solution)/shard_map/while/body/eval_jaxpr/hrb,nb->hrn/dot_general | solution.py:62
  308.5 2.7 constant_dynamic-slice_fusion.3
  312.6 2.4 copy.44
  314.9 4.5 %fusion.46 = f32[512,32,128]{2,0,1:T(8,128)S(1)} fusion(f32[32,128,16]{1,2,0:T(8,128)} %get-tuple-element.364, s32[512]{0:T(512)} %dynamic_slice.29), kind=kOutput, calls=%fused_computation.13.clone.1 | convolution fusion | flops 402661376 | bytes 8652800 | tf_op jit(solution)/shard_map/while/body/eval_jaxpr/hrb,nb->hrn/dot_general | solution.py:62
  324.6 2.7 constant_dynamic-slice_fusion.3
  328.7 2.4 copy.44
  331.1 4.5 %fusion.46 = f32[512,32,128]{2,0,1:T(8,128)S(1)} fusion(f32[32,128,16]{1,2,0:T(8,128)} %get-tuple-element.364, s32[512]{0:T(512)} %dynamic_slice.29), kind=kOutput, calls=%fused_computation.13.clone.1 | convolution fusion | flops 402661376 | bytes 8652800 | tf_op jit(solution)/shard_map/while/body/eval_jaxpr/hrb,nb->hrn/dot_general | solution.py:62
  340.8 2.7 constant_dynamic-slice_fusion.3
  344.9 2.4 copy.44
  347.2 4.5 %fusion.46 = f32[512,32,128]{2,0,1:T(8,128)S(1)} fusion(f32[32,128,16]{1,2,0:T(8,128)} %get-tuple-element.364, s32[512]{0:T(512)} %dynamic_slice.29), kind=kOutput, calls=%fused_computation.13.clone.1 | convolution fusion | flops 402661376 | bytes 8652800 | tf_op jit(solution)/shard_map/while/body/eval_jaxpr/hrb,nb->hrn/dot_general | solution.py:62
  356.9 2.7 constant_dynamic-slice_fusion.3
  361.0 2.4 copy.44
  363.4 4.5 %fusion.46 = f32[512,32,128]{2,0,1:T(8,128)S(1)} fusion(f32[32,128,16]{1,2,0:T(8,128)} %get-tuple-element.364, s32[512]{0:T(512)} %dynamic_slice.29), kind=kOutput, calls=%fused_computation.13.clone.1 | convolution fusion | flops 402661376 | bytes 8652800 | tf_op jit(solution)/shard_map/while/body/eval_jaxpr/hrb,nb->hrn/dot_general | solution.py:62
  373.1 2.7 constant_dynamic-slice_fusion.3
  377.1 2.4 copy.44
  379.5 4.5 %fusion.46 = f32[512,32,128]{2,0,1:T(8,128)S(1)} fusion(f32[32,128,16]{1,2,0:T(8,128)} %get-tuple-element.364, s32[512]{0:T(512)} %dynamic_slice.29), kind=kOutput, calls=%fused_computation.13.clone.1 | convolution fusion | flops 402661376 | bytes 8652800 | tf_op jit(solution)/shard_map/while/body/eval_jaxpr/hrb,nb->hrn/dot_general | solution.py:62
  389.2 2.7 constant_dynamic-slice_fusion.3
  393.3 2.4 copy.44
  395.7 4.5 %fusion.46 = f32[512,32,128]{2,0,1:T(8,128)S(1)} fusion(f32[32,128,16]{1,2,0:T(8,128)} %get-tuple-element.364, s32[512]{0:T(512)} %dynamic_slice.29), kind=kOutput, calls=%fused_computation.13.clone.1 | convolution fusion | flops 402661376 | bytes 8652800 | tf_op jit(solution)/shard_map/while/body/eval_jaxpr/hrb,nb->hrn/dot_general | solution.py:62
  (189 shorter events, 60.6 us)
Async XLA Ops:
  6.5 129.2 %copy-start = (bf16[768,1536]{1,0:T(8,128)(2,1)S(1)}, bf16[768,1536]{1,0:T(8,128)(2,1)}, u32[]{:S(2)}) copy-start(bf16[768,1536]{1,0:T(8,128)(2,1)} %param.15) | copy-start | bytes 7077892
  6.5 132.9 %copy-start.7 = (f32[32,256]{1,0:T(8,128)S(1)}, f32[32,256]{1,0:T(8,128)}, u32[]{:S(2)}) copy-start(f32[32,256]{1,0:T(8,128)} %param.17) | copy-start | bytes 98308
  6.5 133.0 %copy-start.8 = (s32[128]{0:T(128)S(1)}, s32[128]{0:T(128)}, u32[]{:S(2)}) copy-start(s32[128]{0:T(128)} %param.14) | copy-start | bytes 1540
  6.5 123.5 %all-gather.5.cloned.1.call-start = ((), (), s32[]{:S(2)}) async-start(), calls=%async_computation | async-start | bytes 3342336 | tf_op jit(solution)/shard_map/all_gather | solution.py:20
  7.3 196.3 %all-gather.7.cloned.1.call-start = ((), (), s32[]{:S(2)}) async-start(), calls=%async_computation.1 | async-start | bytes 6488064 | tf_op jit(solution)/shard_map/all_gather | solution.py:41
  137.0 138.5 %all-gather.9.cloned.1.call-start = ((), (), s32[]{:S(2)}) async-start(), calls=%async_computation.2 | async-start | bytes 6488064 | tf_op jit(solution)/shard_map/all_gather | solution.py:42
  275.5 3.3 copy-start.5
  282.7 4.5 %copy-start.2 = (bf16[128,32,24]{0,2,1:T(8,128)(2,1)S(1)}, bf16[128,32,24]{0,2,1:T(8,128)(2,1)}, u32[]{:S(2)}) copy-start(bf16[128,32,24]{0,2,1:T(8,128)(2,1)} %get-tuple-element.362) | copy-start | bytes 589828 | tf_op jit(solution)/shard_map/while
  289.0 1.3 copy-start.3
  289.0 1.3 copy-start.1
  291.7 3.4 copy-start.5
  298.8 4.5 %copy-start.2 = (bf16[128,32,24]{0,2,1:T(8,128)(2,1)S(1)}, bf16[128,32,24]{0,2,1:T(8,128)(2,1)}, u32[]{:S(2)}) copy-start(bf16[128,32,24]{0,2,1:T(8,128)(2,1)} %get-tuple-element.362) | copy-start | bytes 589828 | tf_op jit(solution)/shard_map/while
  305.2 1.3 copy-start.1
  307.8 3.4 copy-start.5
  314.9 4.5 %copy-start.2 = (bf16[128,32,24]{0,2,1:T(8,128)(2,1)S(1)}, bf16[128,32,24]{0,2,1:T(8,128)(2,1)}, u32[]{:S(2)}) copy-start(bf16[128,32,24]{0,2,1:T(8,128)(2,1)} %get-tuple-element.362) | copy-start | bytes 589828 | tf_op jit(solution)/shard_map/while
  321.3 1.3 copy-start.1
  324.0 3.4 copy-start.5
  331.1 4.5 %copy-start.2 = (bf16[128,32,24]{0,2,1:T(8,128)(2,1)S(1)}, bf16[128,32,24]{0,2,1:T(8,128)(2,1)}, u32[]{:S(2)}) copy-start(bf16[128,32,24]{0,2,1:T(8,128)(2,1)} %get-tuple-element.362) | copy-start | bytes 589828 | tf_op jit(solution)/shard_map/while
  337.5 1.3 copy-start.1
  340.1 3.4 copy-start.5
  347.2 4.5 %copy-start.2 = (bf16[128,32,24]{0,2,1:T(8,128)(2,1)S(1)}, bf16[128,32,24]{0,2,1:T(8,128)(2,1)}, u32[]{:S(2)}) copy-start(bf16[128,32,24]{0,2,1:T(8,128)(2,1)} %get-tuple-element.362) | copy-start | bytes 589828 | tf_op jit(solution)/shard_map/while
  353.6 1.3 copy-start.1
  356.2 3.4 copy-start.5
  363.4 4.5 %copy-start.2 = (bf16[128,32,24]{0,2,1:T(8,128)(2,1)S(1)}, bf16[128,32,24]{0,2,1:T(8,128)(2,1)}, u32[]{:S(2)}) copy-start(bf16[128,32,24]{0,2,1:T(8,128)(2,1)} %get-tuple-element.362) | copy-start | bytes 589828 | tf_op jit(solution)/shard_map/while
  369.8 1.3 copy-start.1
  372.4 3.4 copy-start.5
  379.5 4.5 %copy-start.2 = (bf16[128,32,24]{0,2,1:T(8,128)(2,1)S(1)}, bf16[128,32,24]{0,2,1:T(8,128)(2,1)}, u32[]{:S(2)}) copy-start(bf16[128,32,24]{0,2,1:T(8,128)(2,1)} %get-tuple-element.362) | copy-start | bytes 589828 | tf_op jit(solution)/shard_map/while
  385.9 1.3 copy-start.1
  388.5 3.4 copy-start.5
  395.7 4.5 %copy-start.2 = (bf16[128,32,24]{0,2,1:T(8,128)(2,1)S(1)}, bf16[128,32,24]{0,2,1:T(8,128)(2,1)}, u32[]{:S(2)}) copy-start(bf16[128,32,24]{0,2,1:T(8,128)(2,1)} %get-tuple-element.362) | copy-start | bytes 589828 | tf_op jit(solution)/shard_map/while
  402.0 1.3 copy-start.3
  402.0 1.3 copy-start.1
  (22 other events, 28.2 us)
Sparse Core Ops, SparseCore 0:
  10.4 119.6 all-gather.4
  137.1 66.4 all-gather.6
  205.8 69.7 all-gather.8
where the time goes:
time: 414 us; the launch traced here: 413 us
  waiting for transfers between devices  214 us (52%)
  local copies, waits for them, and re-layouts  67.4 us (16%)
  matrix products  65.4 us (16%)
  blocking collectives  39.3 us (9%)
  between operations  13.9 us (3%)
  other arithmetic  11.7 us (3%)
    all_gather x1, waiting for transfers between devices, on_device(): gathered = lax.all_gather(features, 'group', axis=0, tiled=True)  121 us
    all_gather x1, waiting for transfers between devices, on_device(): value_rows = lax.all_gather(values, 'seq', axis=0, tiled=True)  71.9 us
    dynamic_slice x16, local copies, waits for them, and re-layouts, one_block(): lax.dynamic_slice_in_dim(value_rows, offset, key_block, 0)  40.3 us
    all_gather x1, blocking collectives, on_device(): bucket_rows = lax.all_gather(node_bucket, 'seq', axis=0, tiled=True)  39.3 us
    dot_general x8, matrix products, one_block(): jnp.einsum('hrb,nb->hrn', query_bias, onehot, precision=lax.Precision.HIG...  36.1 us
    all_gather x1, waiting for transfers between devices, on_device(): key_rows = lax.all_gather(keys_own, 'seq', axis=0, tiled=True)  19.7 us
    dot_general x8, matrix products, one_block(): jnp.einsum('rhd,nhd->hrn', queries, key_part, preferred_element_type=jnp....  14.7 us
    dynamic_slice x8, local copies, waits for them, and re-layouts, one_block(): lax.dynamic_slice_in_dim(key_rows, offset, key_block, 0)  11.3 us
  transfers between devices with their start and end apart: 3, of which 3 were waited for; matrix products, arithmetic and copies ran while one was open for 2% of the time, Pallas kernels for 0%

commit v1 on v0

v1 whole, which is shorter than its diff:
```python
import functools
import math

import jax
import jax.numpy as jnp
from jax import lax
from jax.experimental import pallas as pl
from jax.experimental.pallas import tpu as pltpu
from jax.sharding import PartitionSpec as P

D = 768
H = 32
HD = 24
NB = 16
TILES = 8
ROWS = 128
NG = 16
NS = 32
NODES_G = ROWS * NS
PIECE = 80
CHUNKS = 4
CROWS = ROWS // CHUNKS
QB = 256
KC = 1024
SCALE_LOG2 = math.log2(math.e) / math.sqrt(HD)
LOG2E = math.log2(math.e)
MESH = pl.DeviceIdType.MESH
F32 = jnp.float32
BF16 = jnp.bfloat16


def aggregate_kernel(
    x_ref, tiles_ref, src_ref, cnt_ref, bucket_ref, wqk_ref, wv_ref,
    out_ref,
    gath, tiles_v, wqk_v, wv_v, qkv_t, send_sem, recv_sem, local_sem,
):
    g = lax.axis_index("group")
    y = g // 4
    z = lax.rem(g, 4)

    def gid(yy, zz):
        return lax.rem(yy, 4) * 4 + lax.rem(zz, 4)

    zp, zm = gid(y, z + 1), gid(y, z + 3)
    yp, ym = gid(y + 1, z), gid(y + 3, z)

    barrier = pltpu.get_barrier_semaphore()
    for peer in (zp, zm, yp, ym):
        pl.semaphore_signal(barrier, inc=1, device_id={"group": peer}, device_id_type=MESH)

    own = pltpu.make_async_copy(x_ref, gath.at[g], local_sem.at[0])
    own.start()
    loads = [
        pltpu.make_async_copy(tiles_ref, tiles_v, local_sem.at[1]),
        pltpu.make_async_copy(wqk_ref, wqk_v, local_sem.at[2]),
        pltpu.make_async_copy(wv_ref, wv_v, local_sem.at[3]),
    ]
    for load in loads:
        load.start()
    pl.semaphore_wait(barrier, 4)

    sent = []

    def block(origin, c):
        return gath.at[origin, pl.ds(c * CROWS, CROWS), :]

    def send(source, origin, c, peer):
        copy = pltpu.make_async_remote_copy(
            src_ref=source,
            dst_ref=block(origin, c),
            send_sem=send_sem.at[len(sent)],
            recv_sem=recv_sem.at[origin, c],
            device_id={"group": peer},
            device_id_type=MESH,
        )
        copy.start()
        sent.append(copy)

    def forward(origin, c, peer):
        send(block(origin, c), origin, c, peer)

    def arrive(origin, c):
        pltpu.make_async_remote_copy(
            src_ref=block(origin, c),
            dst_ref=block(origin, c),
            send_sem=send_sem.at[0],
            recv_sem=recv_sem.at[origin, c],
            device_id={"group": zp},
            device_id_type=MESH,
        ).wait_recv()

    half = CHUNKS // 2
    order = [c for pair in zip(range(half), range(half, CHUNKS)) for c in pair]
    for c in order:
        for peer in (zp, zm):
            send(x_ref.at[pl.ds(c * CROWS, CROWS), :], g, c, peer)
    for c in order:
        for peer in (yp, ym):
            send(x_ref.at[pl.ds(c * CROWS, CROWS), :], g, c, peer)

    def second_y(zz, c):
        if c < half:
            arrive(gid(y + 3, zz), c)
            forward(gid(y + 3, zz), c, yp)
        else:
            arrive(gid(y + 1, zz), c)
            forward(gid(y + 1, zz), c, ym)

    def rest_y(zz, c):
        if c < half:
            arrive(gid(y + 1, zz), c)
        else:
            arrive(gid(y + 3, zz), c)
        arrive(gid(y + 2, zz), c)

    for c in order:
        second_y(z, c)
    behind = None
    for c in order:
        arrive(zm, c)
        if c < half:
            forward(zm, c, zp)
        forward(zm, c, yp)
        forward(zm, c, ym)
        arrive(zp, c)
        if c >= half:
            forward(zp, c, zm)
        forward(zp, c, yp)
        forward(zp, c, ym)
        if behind is not None:
            second_y(z + 1, behind)
            second_y(z + 3, behind)
        behind = c
    z2 = gid(y, z + 2)
    for c in order:
        arrive(z2, c)
        forward(z2, c, yp)
        forward(z2, c, ym)
        if behind is not None:
            second_y(z + 1, behind)
            second_y(z + 3, behind)
            behind = None
    for c in order:
        second_y(z + 2, c)
    own.wait()
    for zz in (z, z + 1, z + 3, z + 2):
        for c in order:
            rest_y(zz, c)
    for load in loads:
        load.wait()

    total = gath[g].astype(F32)
    count = cnt_ref[0]
    for t in range(TILES):
        live = jnp.where(t < count, 1.0, 0.0)
        chosen = gath[src_ref[0, t]]
        part = jnp.dot(
            tiles_v[:, t * ROWS:(t + 1) * ROWS], chosen, preferred_element_type=F32
        )
        total = total + part * live
    mean_square = jnp.mean(total * total, axis=-1, keepdims=True)
    normed = (total * lax.rsqrt(mean_square + 1e-6)).astype(BF16)
    for j in range(3):
        if j < 2:
            weight = wqk_v[:, j * D:(j + 1) * D]
        else:
            weight = wv_v[...]
        res = jnp.dot(normed, weight, preferred_element_type=F32)
        for u in range(D // 128):
            qkv_t[pl.ds(j * D + u * 128, 128), :] = res[:, u * 128:(u + 1) * 128].T
    bucket = jnp.broadcast_to(bucket_ref[...].astype(F32), (8, ROWS))
    for h in range(H):
        parts = [qkv_t[pl.ds(j * D + h * HD, HD), :] for j in range(3)]
        out_ref[h] = jnp.concatenate(parts + [bucket], axis=0).astype(BF16)
    for copy in sent:
        copy.wait_send()


def attention_kernel(
    piece_ref, bias_ref,
    out_ref,
    recv, kaug, qaug_t, vaug_t, s_a, s_b, o_send, o_recv,
    send_sem, recv_sem, osend_sem, orecv_sem, local_sem,
):
    me = lax.axis_index("seq")

    barrier = pltpu.get_barrier_semaphore()

    def greet(k, carry):
        peer = lax.rem(me + k, NS)
        pl.semaphore_signal(barrier, inc=1, device_id={"seq": peer}, device_id_type=MESH)
        return carry

    lax.fori_loop(1, NS, greet, 0)
    pl.semaphore_wait(barrier, NS - 1)

    def piece_copy(peer, slot):
        return pltpu.make_async_remote_copy(
            src_ref=piece_ref.at[peer],
            dst_ref=recv.at[slot],
            send_sem=send_sem.at[peer],
            recv_sem=recv_sem.at[slot],
            device_id={"seq": peer},
            device_id_type=MESH,
        )

    def send_piece(k, carry):
        piece_copy(lax.rem(me + k, NS), me).start()
        return carry

    lax.fori_loop(1, NS, send_piece, 0)
    own = pltpu.make_async_copy(piece_ref.at[me], recv.at[me], local_sem.at[0])
    own.start()

    row = bias_ref[pl.ds(me, 1), :] * LOG2E
    lane = lax.broadcasted_iota(jnp.int32, (NB, NB * NB), 1)
    sub = lax.broadcasted_iota(jnp.int32, (NB, NB * NB), 0)
    spread = jnp.where((lane & (NB - 1)) == sub, jnp.broadcast_to(row, (NB, NB * NB)), 0.0)
    top = spread.astype(BF16)
    left = spread - top.astype(F32)
    mid = left.astype(BF16)
    low = (left - mid.astype(F32)).astype(BF16)
    bias_rows = jnp.concatenate([top, mid, low], axis=0)
    row_bucket = (lax.broadcasted_iota(jnp.int32, (NB * NB, ROWS), 0) >> 4).astype(F32)
    row_index = lax.broadcasted_iota(jnp.int32, (NB, ROWS), 0).astype(F32)
    pad = jnp.zeros((32, ROWS), F32)
    ones = jnp.ones((8, ROWS), F32)

    def prepare(s):
        piece = recv[s].astype(F32)
        q, k, v = piece[0:24] * SCALE_LOG2, piece[24:48], piece[48:72]
        b = piece[72:73]
        q_top = q.astype(BF16).astype(F32)
        chosen = (jnp.broadcast_to(b, (NB * NB, ROWS)) == row_bucket).astype(F32).astype(BF16)
        q_bias = jnp.dot(bias_rows, chosen, preferred_element_type=F32)
        onehot = (jnp.broadcast_to(b, (NB, ROWS)) == row_index).astype(F32)
        off = pl.multiple_of(s * ROWS, ROWS)
        qaug_t[:, pl.ds(off, ROWS)] = jnp.concatenate(
            [q_top, q - q_top, q_bias, pad], axis=0
        ).astype(BF16)
        k_rows = jnp.concatenate([k, k, onehot, onehot, onehot, pad], axis=0)
        kaug[pl.ds(off, ROWS), :] = k_rows.T.astype(BF16)
        vaug_t[:, pl.ds(off, ROWS)] = jnp.concatenate([v, ones], axis=0).astype(BF16)

    own.wait()
    prepare(me)

    def take_piece(k, carry):
        slot = lax.rem(me + NS - k, NS)
        piece_copy(slot, slot).wait_recv()
        prepare(slot)
        return carry

    lax.fori_loop(1, NS, take_piece, 0)

    nq = NODES_G // QB

    def scores(i, j, dest, peak):
        off = pl.multiple_of(i * QB, QB)
        s = jnp.dot(
            kaug[pl.ds(j * KC, KC), :], qaug_t[:, pl.ds(off, QB)], preferred_element_type=F32
        )
        dest[pl.ds(j * KC, KC), :] = s
        return jnp.maximum(peak, jnp.max(s.reshape(KC // 8, 8, QB), axis=0))

    low_peak = jnp.full((8, QB), -3e38, F32)

    def step(i, peak_in, s_in, s_out):
        peak = jnp.max(peak_in, axis=0, keepdims=True)
        after = jnp.minimum(i + 1, nq - 1)
        peak_out = low_peak
        acc = jnp.zeros((32, QB), F32)
        for j in range(NODES_G // KC):
            peak_out = scores(after, j, s_out, peak_out)
            p = jnp.exp2(s_in[pl.ds(j * KC, KC), :] - peak).astype(BF16)
            acc = acc + jnp.dot(
                vaug_t[:, pl.ds(j * KC, KC)], p, preferred_element_type=F32
            )
        res = (acc / acc[24:25]).astype(BF16)
        for u in range(QB // ROWS):
            o_send[i * (QB // ROWS) + u] = res[:, u * ROWS:(u + 1) * ROWS]
        return peak_out

    def out_copy(owner, slot):
        return pltpu.make_async_remote_copy(
            src_ref=o_send.at[owner],
            dst_ref=o_recv.at[slot],
            send_sem=osend_sem.at[owner],
            recv_sem=orecv_sem.at[slot],
            device_id={"seq": owner},
            device_id_type=MESH,
        )

    def give(i):
        for u in range(QB // ROWS):
            owner = i * (QB // ROWS) + u

            @pl.when(owner != me)
            def _():
                out_copy(owner, me).start()

    peak = low_peak
    for j in range(NODES_G // KC):
        peak = scores(0, j, s_a, peak)

    def two(t, peak):
        peak = step(2 * t, peak, s_a, s_b)
        give(2 * t)
        peak = step(2 * t + 1, peak, s_b, s_a)
        give(2 * t + 1)
        return peak

    lax.fori_loop(0, nq // 2, two, peak)
    o_recv[me] = o_send[me]

    def take_out(k, carry):
        slot = lax.rem(me + NS - k, NS)
        out_copy(slot, slot).wait_recv()
        return carry

    lax.fori_loop(1, NS, take_out, 0)
    for h in range(H):
        out_ref[pl.ds(h * HD, HD), :] = o_recv[h].astype(F32)[0:HD]

    def drain(k, carry):
        peer = lax.rem(me + k, NS)
        piece_copy(peer, me).wait_send()
        out_copy(peer, me).wait_send()
        return carry

    lax.fori_loop(1, NS, drain, 0)


def on_device(features, tiles, tile_src, tile_count, node_bucket, w_qk, w_v, bias_table):
    hbm = pl.BlockSpec(memory_space=pl.ANY)
    vmem = pl.BlockSpec(memory_space=pltpu.VMEM)
    smem = pl.BlockSpec(memory_space=pltpu.SMEM)
    sends = 15 * CHUNKS
    pieces = pl.pallas_call(
        aggregate_kernel,
        out_shape=jax.ShapeDtypeStruct((H, PIECE, ROWS), BF16),
        in_specs=[hbm, hbm, smem, smem, vmem, hbm, hbm],
        out_specs=vmem,
        scratch_shapes=[
            pltpu.VMEM((NG, ROWS, D), BF16),
            pltpu.VMEM((ROWS, TILES * ROWS), BF16),
            pltpu.VMEM((D, 2 * D), BF16),
            pltpu.VMEM((D, D), BF16),
            pltpu.VMEM((3 * D, ROWS), F32),
            pltpu.SemaphoreType.DMA((sends,)),
            pltpu.SemaphoreType.DMA((NG, CHUNKS)),
            pltpu.SemaphoreType.DMA((4,)),
        ],
        compiler_params=pltpu.CompilerParams(
            collective_id=0, has_side_effects=True, vmem_limit_bytes=62 * 1024 * 1024
        ),
        name="aggregate",
    )(features, tiles, tile_src, tile_count, node_bucket.reshape(1, ROWS), w_qk, w_v)
    out_t = pl.pallas_call(
        attention_kernel,
        out_shape=jax.ShapeDtypeStruct((D, ROWS), F32),
        in_specs=[hbm, vmem],
        out_specs=vmem,
        scratch_shapes=[
            pltpu.VMEM((NS, PIECE, ROWS), BF16),
            pltpu.VMEM((NODES_G, 128), BF16),
            pltpu.VMEM((128, NODES_G), BF16),
            pltpu.VMEM((32, NODES_G), BF16),
            pltpu.VMEM((NODES_G, QB), F32),
            pltpu.VMEM((NODES_G, QB), F32),
            pltpu.VMEM((NS, 32, ROWS), BF16),
            pltpu.VMEM((NS, 32, ROWS), BF16),
            pltpu.SemaphoreType.DMA((NS,)),
            pltpu.SemaphoreType.DMA((NS,)),
            pltpu.SemaphoreType.DMA((NS,)),
            pltpu.SemaphoreType.DMA((NS,)),
            pltpu.SemaphoreType.DMA((1,)),
        ],
        compiler_params=pltpu.CompilerParams(
            collective_id=1, has_side_effects=True, vmem_limit_bytes=56 * 1024 * 1024
        ),
        name="attention",
    )(pieces, bias_table)
    return out_t.T.astype(BF16)


def solution(mesh):
    rows = P(("group", "seq"), None)
    line = P(("group", "seq"))
    return jax.shard_map(
        on_device,
        mesh=mesh,
        in_specs=(rows, rows, rows, line, line, P(), P(), P()),
        out_specs=rows,
        check_vma=False,
    )
```

time: 414 us -> 103 us (0.25)
  waiting for transfers between devices: 214 us -> 0 us
  Pallas kernels: 0 us -> 99 us
  local copies, waits for them, and re-layouts: 67.4 us -> 0.83 us
  matrix products: 65.4 us -> 0 us
  blocking collectives: 39.3 us -> 0 us
  between operations: 13.9 us -> 0.67 us
  other arithmetic: 11.7 us -> 1.02 us
    all_gather x3 -> x0, waiting for transfers between devices: 213 us -> none  [the longest x1 121 us: on_device(): gathered = lax.all_gather(features, 'group', axis=0, tiled=True)]
    pallas_call x0 -> x2, Pallas kernels: none -> 99 us  [the longest x1 51.6 us: on_device(): pl.pallas_call(aggregate_kernel, out_shape=jax.ShapeDtypeStruct((H, PIECE...]
    dot_general x27 -> x0, matrix products: 65.4 us -> none  [the longest x8 36.1 us: one_block(): jnp.einsum('hrb,nb->hrn', query_bias, onehot, precision=lax.Precision.HIG...]
    dynamic_slice x32 -> x0, local copies, waits for them, and re-layouts: 56.9 us -> none  [the longest x16 40.3 us: one_block(): lax.dynamic_slice_in_dim(value_rows, offset, key_block, 0)]
    all_gather x1 -> x0, blocking collectives: 39.3 us -> none  [on_device(): bucket_rows = lax.all_gather(node_bucket, 'seq', axis=0, tiled=True)]
    reduce_sum x8 -> x0, other arithmetic: 10.1 us -> none  [one_block(): total_new = total_old * factor + jnp.sum(weights, axis=-1)]
    gather x2 -> x0, local copies, waits for them, and re-layouts: 5.48 us -> none  [the longest x1 3.68 us: on_device(): chosen = gathered.reshape(group_count, row_count, feat_width)[sources]]
  transfers between devices with their start and end apart: 3 -> 0, of which waited for: 3 -> 0; matrix products, arithmetic and copies ran while one was open for 2% -> 0% of each run, Pallas kernels for 0% -> 0%
where the time goes in v1:
time: 103 us; the launch traced here: 101 us
  Pallas kernels  99 us (96%)
    pallas_call x1, Pallas kernels, on_device(): pl.pallas_call(aggregate_kernel, out_shape=jax.ShapeDtypeStruct((H, PIECE...  51.6 us
    pallas_call x1, Pallas kernels, on_device(): pl.pallas_call(attention_kernel, out_shape=jax.ShapeDtypeStruct((D, ROWS)...  47.3 us

profile of v1, /device:TPU:1, one launch (start us, length us, event | category | flops | bytes accessed | tf_op | source)
XLA Modules:
  0.0 101.5 jit_solution(18248297131124492259)
XLA Ops:
  0.7 51.6 %aggregate.1.piece_ref = bf16[32,80,128]{2,1,0:T(8,128)(2,1)} custom-call(bf16[128,768]{1,0:T(8,128)(2,1)} %x_ref.1, bf16[128,1024]{1,0:T(8,128)(2,1)} %tiles_ref.1, s32[1,8]{1,0:T(1,128)} %src_ref.1, s32[1]{0:T(128)S(6)} %copy.10.cnt_ref, s32[1,128]{1,0:T(1,128)} %bitcast.3, bf16[768,1536]{1,0:T(8,128)(2,1)} %wqk_ref.1, bf16[768,768]{1,0:T(8,128)(2,1)} %wv_ref.1), custom_call_target="tpu_custom_call" | custom-call | tf_op jit(solution)/shard_map/aggregate/pallas_call | solution.py:339
  52.3 47.3 %attention.1 = f32[768,128]{1,0:T(8,128)} custom-call(bf16[32,80,128]{2,1,0:T(8,128)(2,1)} %aggregate.1.piece_ref, f32[32,256]{1,0:T(8,128)} %bias_ref.1), custom_call_target="tpu_custom_call" | custom-call | tf_op jit(solution)/shard_map/attention/pallas_call | solution.py:359
  99.6 1.0 %convert_bitcast_fusion = bf16[128,768]{0,1:T(8,128)(2,1)S(1)} fusion(f32[768,128]{1,0:T(8,128)} %attention.1), kind=kLoop, calls=%fused_computation | loop fusion | flops 98304 | bytes 589824 | tf_op jit(solution)/shard_map/convert_element_type | solution.py:384
  100.6 0.8 copy.9

commit v2 on v1

v2 whole, which is shorter than its diff:
```python
import functools
import math

import jax
import jax.numpy as jnp
from jax import lax
from jax.experimental import pallas as pl
from jax.experimental.pallas import tpu as pltpu
from jax.sharding import PartitionSpec as P

D = 768
H = 32
HD = 24
NB = 16
TILES = 8
ROWS = 128
NG = 16
NS = 32
NODES_G = ROWS * NS
KROWS = 32
CHUNKS = 4
CROWS = ROWS // CHUNKS
QB = 256
KC = 1024
SCALE_LOG2 = math.log2(math.e) / math.sqrt(HD)
LOG2E = math.log2(math.e)
MESH = pl.DeviceIdType.MESH
F32 = jnp.float32
BF16 = jnp.bfloat16


def layer_kernel(
    x_ref, tiles_ref, src_ref, cnt_ref, bucket_ref, wqk_ref, wv_ref, bias_ref,
    out_ref,
    gath, tiles_v, wqk_v, wv_v, qkv_t,
    k_send, v_send, q_send, k_recv, v_recv, q_recv, o_send, o_recv,
    kaug, vaug_t, q_even, q_odd, s_even, s_odd,
    gsend_sem, grecv_sem, local_sem,
    ksend_sem, krecv_sem, vsend_sem, vrecv_sem, qsend_sem, qrecv_sem, osend_sem, orecv_sem,
):
    g = lax.axis_index("group")
    me = lax.axis_index("seq")
    y = g // 4
    z = lax.rem(g, 4)

    def gid(yy, zz):
        return lax.rem(yy, 4) * 4 + lax.rem(zz, 4)

    zp, zm = gid(y, z + 1), gid(y, z + 3)
    yp, ym = gid(y + 1, z), gid(y + 3, z)

    barrier = pltpu.get_barrier_semaphore()
    for peer in (zp, zm, yp, ym):
        pl.semaphore_signal(barrier, inc=1, device_id={"group": peer}, device_id_type=MESH)

    def greet(k, carry):
        peer = lax.rem(me + k, NS)
        pl.semaphore_signal(barrier, inc=1, device_id={"seq": peer}, device_id_type=MESH)
        return carry

    lax.fori_loop(1, NS, greet, 0)

    own = pltpu.make_async_copy(x_ref, gath.at[g], local_sem.at[0])
    own.start()
    loads = [
        pltpu.make_async_copy(tiles_ref, tiles_v, local_sem.at[1]),
        pltpu.make_async_copy(wqk_ref, wqk_v, local_sem.at[2]),
        pltpu.make_async_copy(wv_ref, wv_v, local_sem.at[3]),
    ]
    for load in loads:
        load.start()
    pl.semaphore_wait(barrier, 4 + NS - 1)

    sent = []

    def block(origin, c):
        return gath.at[origin, pl.ds(c * CROWS, CROWS), :]

    def send(source, origin, c, peer):
        copy = pltpu.make_async_remote_copy(
            src_ref=source,
            dst_ref=block(origin, c),
            send_sem=gsend_sem.at[len(sent)],
            recv_sem=grecv_sem.at[origin, c],
            device_id={"group": peer},
            device_id_type=MESH,
        )
        copy.start()
        sent.append(copy)

    def first(c, peer):
        send(x_ref.at[pl.ds(c * CROWS, CROWS), :], g, c, peer)

    def forward(origin, c, peer):
        send(block(origin, c), origin, c, peer)

    arrived = set()

    def arrive(dy, dz, c):
        arrived.add((dy, dz, c))
        origin = gid(y + dy, z + dz)
        pltpu.make_async_remote_copy(
            src_ref=block(origin, c),
            dst_ref=block(origin, c),
            send_sem=gsend_sem.at[0],
            recv_sem=grecv_sem.at[origin, c],
            device_id={"group": zp},
            device_id_type=MESH,
        ).wait_recv()

    half = CHUNKS // 2
    upper = list(range(half))
    lower = list(range(CHUNKS - 1, half - 1, -1))
    pending = []

    def across(dz, c):
        forward(gid(y, z + dz), c, yp)
        forward(gid(y, z + dz), c, ym)
        pending.append((dz, c))

    def catch_up(keep):
        while len(pending) > keep:
            dz, c = pending.pop(0)
            dy, peer = (3, yp) if c < half else (1, ym)
            arrive(dy, dz, c)
            forward(gid(y + dy, z + dz), c, peer)

    for t, b in zip(upper, lower):
        first(b, zp)
        first(t, zm)
    for t, b in zip(upper, lower):
        first(t, zp)
        first(b, zm)
    for t, b in zip(upper, lower):
        for c in (t, b):
            first(c, yp)
            first(c, ym)
            pending.append((0, c))
    for t, b in zip(upper, lower):
        arrive(0, 3, b)
        across(3, b)
        arrive(0, 1, t)
        across(1, t)
        catch_up(2)
    for t, b in zip(upper, lower):
        arrive(0, 3, t)
        forward(zm, t, zp)
        arrive(0, 1, b)
        forward(zp, b, zm)
        across(3, t)
        across(1, b)
        catch_up(2)
    for t, b in zip(upper, lower):
        arrive(0, 2, t)
        across(2, t)
        arrive(0, 2, b)
        across(2, b)
        catch_up(2)
    catch_up(0)
    own.wait()
    for load in loads:
        load.wait()
    for dz in (0, 1, 3, 2):
        for dy in (1, 3, 2):
            for c in range(CHUNKS):
                if (dy, dz, c) not in arrived:
                    arrive(dy, dz, c)

    total = gath[g].astype(F32)
    count = cnt_ref[0]
    for t in range(TILES):
        live = jnp.where(t < count, 1.0, 0.0)
        chosen = gath[src_ref[0, t]]
        part = jnp.dot(
            tiles_v[:, t * ROWS:(t + 1) * ROWS], chosen, preferred_element_type=F32
        )
        total = total + part * live
    mean_square = jnp.mean(total * total, axis=-1, keepdims=True)
    normed = (total * lax.rsqrt(mean_square + 1e-6)).astype(BF16)
    bucket = jnp.broadcast_to(bucket_ref[...].astype(F32), (8, ROWS))

    def exchange(source, dest, send_sem, recv_sem):
        def copy(peer, slot):
            return pltpu.make_async_remote_copy(
                src_ref=source.at[peer],
                dst_ref=dest.at[slot],
                send_sem=send_sem.at[peer],
                recv_sem=recv_sem.at[slot],
                device_id={"seq": peer},
                device_id_type=MESH,
            )

        return copy

    k_copy = exchange(k_send, k_recv, ksend_sem, krecv_sem)
    v_copy = exchange(v_send, v_recv, vsend_sem, vrecv_sem)
    q_copy = exchange(q_send, q_recv, qsend_sem, qrecv_sem)
    o_copy = exchange(o_send, o_recv, osend_sem, orecv_sem)

    def project(weight, dest, recv, copy, extra):
        res = jnp.dot(normed, weight, preferred_element_type=F32)
        for u in range(D // 128):
            qkv_t[pl.ds(u * 128, 128), :] = res[:, u * 128:(u + 1) * 128].T
        for h in range(H):
            rows = qkv_t[pl.ds(h * HD, HD), :]
            if extra is not None:
                rows = jnp.concatenate([rows, extra], axis=0)
            dest[h] = rows.astype(BF16)

        def scatter(k, carry):
            copy(lax.rem(me + k, NS), me).start()
            return carry

        lax.fori_loop(1, NS, scatter, 0)
        recv[me] = dest[me]

    project(wqk_v[:, D:2 * D], k_send, k_recv, k_copy, bucket)
    project(wv_v[...], v_send, v_recv, v_copy, None)
    project(wqk_v[:, 0:D], q_send, q_recv, q_copy, None)

    row = bias_ref[pl.ds(me, 1), :] * LOG2E
    lane = lax.broadcasted_iota(jnp.int32, (NB, NB * NB), 1)
    sub = lax.broadcasted_iota(jnp.int32, (NB, NB * NB), 0)
    spread = jnp.where((lane & (NB - 1)) == sub, jnp.broadcast_to(row, (NB, NB * NB)), 0.0)
    top = spread.astype(BF16)
    left = spread - top.astype(F32)
    mid = left.astype(BF16)
    low = (left - mid.astype(F32)).astype(BF16)
    bias_rows = jnp.concatenate([top, mid, low], axis=0)
    row_bucket = (lax.broadcasted_iota(jnp.int32, (NB * NB, ROWS), 0) >> 4).astype(F32)
    row_index = lax.broadcasted_iota(jnp.int32, (NB, ROWS), 0).astype(F32)
    pad = jnp.zeros((32, ROWS), F32)
    ones = jnp.ones((8, ROWS), F32)

    def prepare_kv(s):
        k_piece = k_recv[s].astype(F32)
        k, b = k_piece[0:HD], k_piece[HD:HD + 1]
        onehot = (jnp.broadcast_to(b, (NB, ROWS)) == row_index).astype(F32)
        off = pl.multiple_of(s * ROWS, ROWS)
        k_rows = jnp.concatenate([k, k, onehot, onehot, onehot, pad], axis=0)
        kaug[pl.ds(off, ROWS), :] = k_rows.T.astype(BF16)
        v = v_recv[s].astype(F32)
        vaug_t[:, pl.ds(off, ROWS)] = jnp.concatenate([v, ones], axis=0).astype(BF16)

    def take_kv(k, carry):
        slot = lax.rem(me + NS - k, NS)
        k_copy(slot, slot).wait_recv()
        v_copy(slot, slot).wait_recv()
        prepare_kv(slot)
        return carry

    prepare_kv(me)
    lax.fori_loop(1, NS, take_kv, 0)

    nq = NODES_G // QB
    per = QB // ROWS
    start = me // per

    def owner_of(i, u):
        return lax.rem(start + i, nq) * per + u

    def wait_q(i):
        for u in range(per):
            slot = owner_of(i, u)

            @pl.when((slot != me) & (i < nq))
            def _():
                q_copy(slot, slot).wait_recv()

    def prepare_q(i, dest):
        for u in range(per):
            slot = owner_of(i, u)
            q = q_recv[slot].astype(F32) * SCALE_LOG2
            b = k_recv[slot].astype(F32)[HD:HD + 1]
            q_top = q.astype(BF16).astype(F32)
            chosen = (jnp.broadcast_to(b, (NB * NB, ROWS)) == row_bucket).astype(F32)
            q_bias = jnp.dot(bias_rows, chosen.astype(BF16), preferred_element_type=F32)
            dest[:, u * ROWS:(u + 1) * ROWS] = jnp.concatenate(
                [q_top, q - q_top, q_bias, pad], axis=0
            ).astype(BF16)

    def scores(j, q_now, dest, peak):
        s = jnp.dot(kaug[pl.ds(j * KC, KC), :], q_now[...], preferred_element_type=F32)
        dest[pl.ds(j * KC, KC), :] = s
        return jnp.maximum(peak, jnp.max(s.reshape(KC // 8, 8, QB), axis=0))

    low_peak = jnp.full((8, QB), -3e38, F32)

    def step(i, peak_in, s_in, s_out, q_after, q_later):
        wait_q(i + 2)
        peak = jnp.max(peak_in, axis=0, keepdims=True)
        peak_out = low_peak
        acc = jnp.zeros((32, QB), F32)
        for j in range(NODES_G // KC):
            peak_out = scores(j, q_after, s_out, peak_out)
            p = jnp.exp2(s_in[pl.ds(j * KC, KC), :] - peak).astype(BF16)
            acc = acc + jnp.dot(
                vaug_t[:, pl.ds(j * KC, KC)], p, preferred_element_type=F32
            )
        prepare_q(i + 2, q_later)
        res = (acc[0:HD] / acc[HD:HD + 1]).astype(BF16)
        for u in range(per):
            o_send[owner_of(i, u)] = res[:, u * ROWS:(u + 1) * ROWS]
        for u in range(per):
            owner = owner_of(i, u)

            @pl.when(owner != me)
            def _():
                o_copy(owner, me).start()

        return peak_out

    wait_q(0)
    wait_q(1)
    prepare_q(0, q_even)
    prepare_q(1, q_odd)
    peak = low_peak
    for j in range(NODES_G // KC):
        peak = scores(j, q_even, s_even, peak)

    def two(t, peak):
        peak = step(2 * t, peak, s_even, s_odd, q_odd, q_even)
        return step(2 * t + 1, peak, s_odd, s_even, q_even, q_odd)

    lax.fori_loop(0, nq // 2, two, peak)
    o_recv[me] = o_send[me]

    def take_out(k, carry):
        slot = lax.rem(me + NS - k, NS)
        o_copy(slot, slot).wait_recv()
        return carry

    lax.fori_loop(1, NS, take_out, 0)
    for h in range(H):
        qkv_t[pl.ds(h * HD, HD), :] = o_recv[h].astype(F32)
    for u in range(D // 128):
        out_ref[:, u * 128:(u + 1) * 128] = qkv_t[pl.ds(u * 128, 128), :].T.astype(BF16)

    def drain(k, carry):
        peer = lax.rem(me + k, NS)
        for copy in (k_copy, v_copy, q_copy, o_copy):
            copy(peer, me).wait_send()
        return carry

    lax.fori_loop(1, NS, drain, 0)
    for copy in sent:
        copy.wait_send()


def on_device(features, tiles, tile_src, tile_count, node_bucket, w_qk, w_v, bias_table):
    hbm = pl.BlockSpec(memory_space=pl.ANY)
    vmem = pl.BlockSpec(memory_space=pltpu.VMEM)
    smem = pl.BlockSpec(memory_space=pltpu.SMEM)
    dma = pltpu.SemaphoreType.DMA
    return pl.pallas_call(
        layer_kernel,
        out_shape=jax.ShapeDtypeStruct((ROWS, D), BF16),
        in_specs=[hbm, hbm, smem, smem, vmem, hbm, hbm, vmem],
        out_specs=vmem,
        scratch_shapes=[
            pltpu.VMEM((NG, ROWS, D), BF16),
            pltpu.VMEM((ROWS, TILES * ROWS), BF16),
            pltpu.VMEM((D, 2 * D), BF16),
            pltpu.VMEM((D, D), BF16),
            pltpu.VMEM((D, ROWS), F32),
            pltpu.VMEM((NS, KROWS, ROWS), BF16),
            pltpu.VMEM((NS, HD, ROWS), BF16),
            pltpu.VMEM((NS, HD, ROWS), BF16),
            pltpu.VMEM((NS, KROWS, ROWS), BF16),
            pltpu.VMEM((NS, HD, ROWS), BF16),
            pltpu.VMEM((NS, HD, ROWS), BF16),
            pltpu.VMEM((NS, HD, ROWS), BF16),
            pltpu.VMEM((NS, HD, ROWS), BF16),
            pltpu.VMEM((NODES_G, 128), BF16),
            pltpu.VMEM((32, NODES_G), BF16),
            pltpu.VMEM((128, QB), BF16),
            pltpu.VMEM((128, QB), BF16),
            pltpu.VMEM((NODES_G, QB), F32),
            pltpu.VMEM((NODES_G, QB), F32),
            dma((15 * CHUNKS,)),
            dma((NG, CHUNKS)),
            dma((4,)),
        ] + [dma((NS,)) for _ in range(8)],
        compiler_params=pltpu.CompilerParams(
            collective_id=0, has_side_effects=True, vmem_limit_bytes=62 * 1024 * 1024
        ),
        name="layer",
    )(features, tiles, tile_src, tile_count, node_bucket.reshape(1, ROWS), w_qk, w_v, bias_table)


def solution(mesh):
    rows = P(("group", "seq"), None)
    line = P(("group", "seq"))
    return jax.shard_map(
        on_device,
        mesh=mesh,
        in_specs=(rows, rows, rows, line, line, P(), P(), P()),
        out_specs=rows,
        check_vma=False,
    )
```

time: 103 us -> 96.7 us (0.939); the launches traced: 101 us -> 96.5 us
  Pallas kernels: 99 us -> 94.2 us
    pallas_call x2 -> x1, Pallas kernels: 99 us -> 94.2 us  [on_device(): pl.pallas_call(layer_kernel, out_shape=jax.ShapeDtypeStruct((ROWS, D), BF...]
    unnamed x0 -> x1, local copies, waits for them, and re-layouts: none -> 1.62 us
where the time goes in v2:
time: 96.7 us; the launch traced here: 96.5 us
  Pallas kernels  94.2 us (97%)
  local copies, waits for them, and re-layouts  1.62 us (2%)
    pallas_call x1, Pallas kernels, on_device(): pl.pallas_call(layer_kernel, out_shape=jax.ShapeDtypeStruct((ROWS, D), BF...  94.2 us

profile of v2, /device:TPU:1, one launch (start us, length us, event | category | flops | bytes accessed | tf_op | source)
XLA Modules:
  0.0 96.5 jit_solution(4175700551297617326)
XLA Ops:
  0.7 94.2 %layer.1 = bf16[128,768]{1,0:T(8,128)(2,1)} custom-call(bf16[128,768]{1,0:T(8,128)(2,1)} %x_ref.1, bf16[128,1024]{1,0:T(8,128)(2,1)} %tiles_ref.1, s32[1,8]{1,0:T(1,128)} %src_ref.1, s32[1]{0:T(128)S(6)} %copy.10.cnt_ref, s32[1,128]{1,0:T(1,128)} %bitcast.1, bf16[768,1536]{1,0:T(8,128)(2,1)} %wqk_ref.1, bf16[768,768]{1,0:T(8,128)(2,1)} %wv_ref.1, ...), custom_call_target="tpu_custom_call" | custom-call | tf_op jit(solution)/shard_map/layer/pallas_call | solution.py:355
  94.9 1.6 %copy.11 = bf16[128,768]{1,0:T(8,128)(2,1)} copy(bf16[128,768]{1,0:T(8,128)(2,1)} %layer.1) | data formatting | bytes 393216

commit v3 on v2

--- a/solution.py
+++ b/solution.py
@@ -17,7 +17,7 @@
 NG = 16
 NS = 32
 NODES_G = ROWS * NS
-KROWS = 32
+HELD = 8
 CHUNKS = 4
 CROWS = ROWS // CHUNKS
 QB = 256
@@ -33,9 +33,9 @@
     x_ref, tiles_ref, src_ref, cnt_ref, bucket_ref, wqk_ref, wv_ref, bias_ref,
     out_ref,
     gath, tiles_v, wqk_v, wv_v, qkv_t,
-    k_send, v_send, q_send, k_recv, v_recv, q_recv, o_send, o_recv,
-    kaug, vaug_t, q_even, q_odd, s_even, s_odd,
-    gsend_sem, grecv_sem, local_sem,
+    b_recv, k_send, v_send, q_send, k_recv, v_recv, q_recv, o_send, o_recv,
+    kaug, vaug_t, q_all, s_all, peaks,
+    gsend_sem, grecv_sem, local_sem, bsend_sem, brecv_sem,
     ksend_sem, krecv_sem, vsend_sem, vrecv_sem, qsend_sem, qrecv_sem, osend_sem, orecv_sem,
 ):
     g = lax.axis_index("group")
@@ -136,6 +136,23 @@
             first(c, yp)
             first(c, ym)
             pending.append((0, c))
+
+    def b_copy(peer, slot):
+        return pltpu.make_async_remote_copy(
+            src_ref=bucket_ref,
+            dst_ref=b_recv.at[slot],
+            send_sem=bsend_sem.at[peer],
+            recv_sem=brecv_sem.at[slot],
+            device_id={"seq": peer},
+            device_id_type=MESH,
+        )
+
+    def send_bucket(k, carry):
+        b_copy(lax.rem(me + k, NS), me).start()
+        return carry
+
+    lax.fori_loop(1, NS, send_bucket, 0)
+    b_recv[me] = bucket_ref[...]
     for t, b in zip(upper, lower):
         arrive(0, 3, b)
         across(3, b)
@@ -177,7 +194,6 @@
         total = total + part * live
     mean_square = jnp.mean(total * total, axis=-1, keepdims=True)
     normed = (total * lax.rsqrt(mean_square + 1e-6)).astype(BF16)
-    bucket = jnp.broadcast_to(bucket_ref[...].astype(F32), (8, ROWS))
 
     def exchange(source, dest, send_sem, recv_sem):
         def copy(peer, slot):
@@ -197,26 +213,23 @@
     q_copy = exchange(q_send, q_recv, qsend_sem, qrecv_sem)
     o_copy = exchange(o_send, o_recv, osend_sem, orecv_sem)
 
-    def project(weight, dest, recv, copy, extra):
+    def project(weight, dest, recv, copy, sign):
         res = jnp.dot(normed, weight, preferred_element_type=F32)
         for u in range(D // 128):
             qkv_t[pl.ds(u * 128, 128), :] = res[:, u * 128:(u + 1) * 128].T
         for h in range(H):
-            rows = qkv_t[pl.ds(h * HD, HD), :]
-            if extra is not None:
-                rows = jnp.concatenate([rows, extra], axis=0)
-            dest[h] = rows.astype(BF16)
+            dest[h] = qkv_t[pl.ds(h * HD, HD), :].astype(BF16)
 
         def scatter(k, carry):
-            copy(lax.rem(me + k, NS), me).start()
+            copy(lax.rem(me + NS + sign * k, NS), me).start()
             return carry
 
         lax.fori_loop(1, NS, scatter, 0)
         recv[me] = dest[me]
 
-    project(wqk_v[:, D:2 * D], k_send, k_recv, k_copy, bucket)
-    project(wv_v[...], v_send, v_recv, v_copy, None)
-    project(wqk_v[:, 0:D], q_send, q_recv, q_copy, None)
+    project(wqk_v[:, D:2 * D], k_send, k_recv, k_copy, 1)
+    project(wqk_v[:, 0:D], q_send, q_recv, q_copy, -1)
+    project(wv_v[...], v_send, v_recv, v_copy, 1)
 
     row = bias_ref[pl.ds(me, 1), :] * LOG2E
     lane = lax.broadcasted_iota(jnp.int32, (NB, NB * NB), 1)
@@ -230,27 +243,23 @@
     row_bucket = (lax.broadcasted_iota(jnp.int32, (NB * NB, ROWS), 0) >> 4).astype(F32)
     row_index = lax.broadcasted_iota(jnp.int32, (NB, ROWS), 0).astype(F32)
     pad = jnp.zeros((32, ROWS), F32)
-    ones = jnp.ones((8, ROWS), F32)
-
-    def prepare_kv(s):
-        k_piece = k_recv[s].astype(F32)
-        k, b = k_piece[0:HD], k_piece[HD:HD + 1]
-        onehot = (jnp.broadcast_to(b, (NB, ROWS)) == row_index).astype(F32)
+
+    def prepare_k(s):
+        k = k_recv[s].astype(F32)
+        onehot = (jnp.broadcast_to(b_recv[s].astype(F32), (NB, ROWS)) == row_index).astype(F32)
         off = pl.multiple_of(s * ROWS, ROWS)
         k_rows = jnp.concatenate([k, k, onehot, onehot, onehot, pad], axis=0)
         kaug[pl.ds(off, ROWS), :] = k_rows.T.astype(BF16)
-        v = v_recv[s].astype(F32)
-        vaug_t[:, pl.ds(off, ROWS)] = jnp.concatenate([v, ones], axis=0).astype(BF16)
-
-    def take_kv(k, carry):
+
+    def take_k(k, carry):
         slot = lax.rem(me + NS - k, NS)
+        b_copy(slot, slot).wait_recv()
         k_copy(slot, slot).wait_recv()
-        v_copy(slot, slot).wait_recv()
-        prepare_kv(slot)
-        return carry
-
-    prepare_kv(me)
-    lax.fori_loop(1, NS, take_kv, 0)
+        prepare_k(slot)
+        return carry
+
+    prepare_k(me)
+    lax.fori_loop(1, NS, take_k, 0)
 
     nq = NODES_G // QB
     per = QB // ROWS
@@ -267,37 +276,50 @@
             def _():
                 q_copy(slot, slot).wait_recv()
 
-    def prepare_q(i, dest):
+    def prepare_q(i):
         for u in range(per):
             slot = owner_of(i, u)
             q = q_recv[slot].astype(F32) * SCALE_LOG2
-            b = k_recv[slot].astype(F32)[HD:HD + 1]
+            b = b_recv[slot].astype(F32)
             q_top = q.astype(BF16).astype(F32)
             chosen = (jnp.broadcast_to(b, (NB * NB, ROWS)) == row_bucket).astype(F32)
             q_bias = jnp.dot(bias_rows, chosen.astype(BF16), preferred_element_type=F32)
-            dest[:, u * ROWS:(u + 1) * ROWS] = jnp.concatenate(
+            q_all[i, :, u * ROWS:(u + 1) * ROWS] = jnp.concatenate(
                 [q_top, q - q_top, q_bias, pad], axis=0
             ).astype(BF16)
 
-    def scores(j, q_now, dest, peak):
-        s = jnp.dot(kaug[pl.ds(j * KC, KC), :], q_now[...], preferred_element_type=F32)
-        dest[pl.ds(j * KC, KC), :] = s
+    low_peak = jnp.full((8, QB), -3e38, F32)
+
+    def scores(i, j, slot, peak):
+        s = jnp.dot(kaug[pl.ds(j * KC, KC), :], q_all[i], preferred_element_type=F32)
+        s_all[slot, pl.ds(j * KC, KC), :] = s
         return jnp.maximum(peak, jnp.max(s.reshape(KC // 8, 8, QB), axis=0))
 
-    low_peak = jnp.full((8, QB), -3e38, F32)
-
-    def step(i, peak_in, s_in, s_out, q_after, q_later):
-        wait_q(i + 2)
-        peak = jnp.max(peak_in, axis=0, keepdims=True)
+    def early(i, carry):
+        wait_q(i + 1)
+        peak = low_peak
+        for j in range(NODES_G // KC):
+            peak = scores(i, j, i, peak)
+        prepare_q(i + 1)
+        peaks[i] = peak
+        return carry
+
+    def step(i, slot, after):
+        if after:
+            wait_q(i + HELD + 1)
+        peak = jnp.max(peaks[i], axis=0, keepdims=True) - 2.0
         peak_out = low_peak
         acc = jnp.zeros((32, QB), F32)
         for j in range(NODES_G // KC):
-            peak_out = scores(j, q_after, s_out, peak_out)
-            p = jnp.exp2(s_in[pl.ds(j * KC, KC), :] - peak).astype(BF16)
+            p = jnp.exp2((s_all[slot, pl.ds(j * KC, KC), :] - peak).astype(BF16))
             acc = acc + jnp.dot(
                 vaug_t[:, pl.ds(j * KC, KC)], p, preferred_element_type=F32
             )
-        prepare_q(i + 2, q_later)
+            if after:
+                peak_out = scores(i + HELD, j, slot, peak_out)
+        if after:
+            prepare_q(i + HELD + 1)
+            peaks[i + HELD] = peak_out
         res = (acc[0:HD] / acc[HD:HD + 1]).astype(BF16)
         for u in range(per):
             o_send[owner_of(i, u)] = res[:, u * ROWS:(u + 1) * ROWS]
@@ -308,21 +330,32 @@
             def _():
                 o_copy(owner, me).start()
 
-        return peak_out
+    def with_scores(i, carry):
+        step(i, i, True)
+        return carry
+
+    def without_scores(i, carry):
+        step(i, i - HELD, False)
+        return carry
+
+    def place_v(s):
+        off = pl.multiple_of(s * ROWS, ROWS)
+        vaug_t[0:HD, pl.ds(off, ROWS)] = v_recv[s]
+
+    def take_v(k, carry):
+        slot = lax.rem(me + NS - k, NS)
+        v_copy(slot, slot).wait_recv()
+        place_v(slot)
+        return carry
 
     wait_q(0)
-    wait_q(1)
-    prepare_q(0, q_even)
-    prepare_q(1, q_odd)
-    peak = low_peak
-    for j in range(NODES_G // KC):
-        peak = scores(j, q_even, s_even, peak)
-
-    def two(t, peak):
-        peak = step(2 * t, peak, s_even, s_odd, q_odd, q_even)
-        return step(2 * t + 1, peak, s_odd, s_even, q_even, q_odd)
-
-    lax.fori_loop(0, nq // 2, two, peak)
+    prepare_q(0)
+    lax.fori_loop(0, HELD, early, 0)
+    vaug_t[...] = jnp.ones((32, NODES_G), BF16)
+    place_v(me)
+    lax.fori_loop(1, NS, take_v, 0)
+    lax.fori_loop(0, nq - HELD, with_scores, 0)
+    lax.fori_loop(nq - HELD, nq, without_scores, 0)
     o_recv[me] = o_send[me]
 
     def take_out(k, carry):
@@ -338,7 +371,7 @@
 
     def drain(k, carry):
         peer = lax.rem(me + k, NS)
-        for copy in (k_copy, v_copy, q_copy, o_copy):
+        for copy in (b_copy, k_copy, v_copy, q_copy, o_copy):
             copy(peer, me).wait_send()
         return carry
 
@@ -363,24 +396,17 @@
             pltpu.VMEM((D, 2 * D), BF16),
             pltpu.VMEM((D, D), BF16),
             pltpu.VMEM((D, ROWS), F32),
-            pltpu.VMEM((NS, KROWS, ROWS), BF16),
-            pltpu.VMEM((NS, HD, ROWS), BF16),
-            pltpu.VMEM((NS, HD, ROWS), BF16),
-            pltpu.VMEM((NS, KROWS, ROWS), BF16),
-            pltpu.VMEM((NS, HD, ROWS), BF16),
-            pltpu.VMEM((NS, HD, ROWS), BF16),
-            pltpu.VMEM((NS, HD, ROWS), BF16),
-            pltpu.VMEM((NS, HD, ROWS), BF16),
+            pltpu.VMEM((NS, 1, ROWS), jnp.int32),
+        ] + [pltpu.VMEM((NS, HD, ROWS), BF16) for _ in range(8)] + [
             pltpu.VMEM((NODES_G, 128), BF16),
             pltpu.VMEM((32, NODES_G), BF16),
-            pltpu.VMEM((128, QB), BF16),
-            pltpu.VMEM((128, QB), BF16),
-            pltpu.VMEM((NODES_G, QB), F32),
-            pltpu.VMEM((NODES_G, QB), F32),
+            pltpu.VMEM((NODES_G // QB + 1, 128, QB), BF16),
+            pltpu.VMEM((HELD, NODES_G, QB), F32),
+            pltpu.VMEM((NODES_G // QB, 8, QB), F32),
             dma((15 * CHUNKS,)),
             dma((NG, CHUNKS)),
             dma((4,)),
-        ] + [dma((NS,)) for _ in range(8)],
+        ] + [dma((NS,)) for _ in range(10)],
         compiler_params=pltpu.CompilerParams(
             collective_id=0, has_side_effects=True, vmem_limit_bytes=62 * 1024 * 1024
         ),

time: 96.7 us -> 95.5 us (0.988)
  Pallas kernels: 94.2 us -> 93 us
    pallas_call x1, Pallas kernels: 94.2 us -> 93 us  [on_device(): pl.pallas_call(layer_kernel, out_shape=jax.ShapeDtypeStruct((ROWS, D), BF...]
where the time goes in v3:
time: 95.5 us; the launch traced here: 95.3 us
  Pallas kernels  93 us (97%)
  local copies, waits for them, and re-layouts  1.62 us (2%)
    pallas_call x1, Pallas kernels, on_device(): pl.pallas_call(layer_kernel, out_shape=jax.ShapeDtypeStruct((ROWS, D), BF...  93 us

profile of v3, /device:TPU:1, one launch (start us, length us, event | category | flops | bytes accessed | tf_op | source)
XLA Modules:
  0.0 95.3 jit_solution(14657926899505239032)
XLA Ops:
  0.7 93.0 %layer.1 = bf16[128,768]{1,0:T(8,128)(2,1)} custom-call(bf16[128,768]{1,0:T(8,128)(2,1)} %x_ref.1, bf16[128,1024]{1,0:T(8,128)(2,1)} %tiles_ref.1, s32[1,8]{1,0:T(1,128)} %src_ref.1, s32[1]{0:T(128)S(6)} %copy.10.cnt_ref, s32[1,128]{1,0:T(1,128)} %bitcast.1, bf16[768,1536]{1,0:T(8,128)(2,1)} %wqk_ref.1, bf16[768,768]{1,0:T(8,128)(2,1)} %wv_ref.1, ...), custom_call_target="tpu_custom_call" | custom-call | tf_op jit(solution)/shard_map/layer/pallas_call | solution.py:388
  93.7 1.6 %copy.11 = bf16[128,768]{1,0:T(8,128)(2,1)} copy(bf16[128,768]{1,0:T(8,128)(2,1)} %layer.1) | data formatting | bytes 393216

commit v4 on v3

--- a/solution.py
+++ b/solution.py
@@ -33,10 +33,10 @@
     x_ref, tiles_ref, src_ref, cnt_ref, bucket_ref, wqk_ref, wv_ref, bias_ref,
     out_ref,
     gath, tiles_v, wqk_v, wv_v, qkv_t,
-    b_recv, k_send, v_send, q_send, k_recv, v_recv, q_recv, o_send, o_recv,
+    b_recv, k_send, k_recv, qv_send, qv_recv, o_send, o_recv,
     kaug, vaug_t, q_all, s_all, peaks,
     gsend_sem, grecv_sem, local_sem, bsend_sem, brecv_sem,
-    ksend_sem, krecv_sem, vsend_sem, vrecv_sem, qsend_sem, qrecv_sem, osend_sem, orecv_sem,
+    ksend_sem, krecv_sem, qvsend_sem, qvrecv_sem, osend_sem, orecv_sem,
 ):
     g = lax.axis_index("group")
     me = lax.axis_index("seq")
@@ -209,27 +209,36 @@
         return copy
 
     k_copy = exchange(k_send, k_recv, ksend_sem, krecv_sem)
-    v_copy = exchange(v_send, v_recv, vsend_sem, vrecv_sem)
-    q_copy = exchange(q_send, q_recv, qsend_sem, qrecv_sem)
+    qv_copy = exchange(qv_send, qv_recv, qvsend_sem, qvrecv_sem)
     o_copy = exchange(o_send, o_recv, osend_sem, orecv_sem)
 
-    def project(weight, dest, recv, copy, sign):
+    def project(weight, base):
         res = jnp.dot(normed, weight, preferred_element_type=F32)
         for u in range(D // 128):
-            qkv_t[pl.ds(u * 128, 128), :] = res[:, u * 128:(u + 1) * 128].T
-        for h in range(H):
-            dest[h] = qkv_t[pl.ds(h * HD, HD), :].astype(BF16)
-
-        def scatter(k, carry):
-            copy(lax.rem(me + NS + sign * k, NS), me).start()
-            return carry
-
-        lax.fori_loop(1, NS, scatter, 0)
-        recv[me] = dest[me]
-
-    project(wqk_v[:, D:2 * D], k_send, k_recv, k_copy, 1)
-    project(wqk_v[:, 0:D], q_send, q_recv, q_copy, -1)
-    project(wv_v[...], v_send, v_recv, v_copy, 1)
+            qkv_t[pl.ds(base + u * 128, 128), :] = res[:, u * 128:(u + 1) * 128].T
+
+    def head_rows(base, h):
+        return qkv_t[pl.ds(base + h * HD, HD), :]
+
+    def send_k(k, carry):
+        k_copy(lax.rem(me + k, NS), me).start()
+        return carry
+
+    def send_qv(k, carry):
+        qv_copy(lax.rem(me + NS - k, NS), me).start()
+        return carry
+
+    project(wqk_v[:, D:2 * D], 0)
+    for h in range(H):
+        k_send[h] = head_rows(0, h).astype(BF16)
+    lax.fori_loop(1, NS, send_k, 0)
+    k_recv[me] = k_send[me]
+    project(wqk_v[:, 0:D], 0)
+    project(wv_v[...], D)
+    for h in range(H):
+        qv_send[h] = jnp.concatenate([head_rows(0, h), head_rows(D, h)], axis=0).astype(BF16)
+    lax.fori_loop(1, NS, send_qv, 0)
+    qv_recv[me] = qv_send[me]
 
     row = bias_ref[pl.ds(me, 1), :] * LOG2E
     lane = lax.broadcasted_iota(jnp.int32, (NB, NB * NB), 1)
@@ -274,12 +283,12 @@
 
             @pl.when((slot != me) & (i < nq))
             def _():
-                q_copy(slot, slot).wait_recv()
+                qv_copy(slot, slot).wait_recv()
 
     def prepare_q(i):
         for u in range(per):
             slot = owner_of(i, u)
-            q = q_recv[slot].astype(F32) * SCALE_LOG2
+            q = qv_recv[slot].astype(F32)[0:HD] * SCALE_LOG2
             b = b_recv[slot].astype(F32)
             q_top = q.astype(BF16).astype(F32)
             chosen = (jnp.broadcast_to(b, (NB * NB, ROWS)) == row_bucket).astype(F32)
@@ -288,6 +297,12 @@
                 [q_top, q - q_top, q_bias, pad], axis=0
             ).astype(BF16)
 
+    def place_v(i):
+        for u in range(per):
+            slot = owner_of(i, u)
+            off = pl.multiple_of(slot * ROWS, ROWS)
+            vaug_t[0:HD, pl.ds(off, ROWS)] = qv_recv[slot].astype(F32)[HD:2 * HD].astype(BF16)
+
     low_peak = jnp.full((8, QB), -3e38, F32)
 
     def scores(i, j, slot, peak):
@@ -301,12 +316,11 @@
         for j in range(NODES_G // KC):
             peak = scores(i, j, i, peak)
         prepare_q(i + 1)
+        place_v(i + 1)
         peaks[i] = peak
         return carry
 
     def step(i, slot, after):
-        if after:
-            wait_q(i + HELD + 1)
         peak = jnp.max(peaks[i], axis=0, keepdims=True) - 2.0
         peak_out = low_peak
         acc = jnp.zeros((32, QB), F32)
@@ -338,22 +352,17 @@
         step(i, i - HELD, False)
         return carry
 
-    def place_v(s):
-        off = pl.multiple_of(s * ROWS, ROWS)
-        vaug_t[0:HD, pl.ds(off, ROWS)] = v_recv[s]
-
-    def take_v(k, carry):
-        slot = lax.rem(me + NS - k, NS)
-        v_copy(slot, slot).wait_recv()
-        place_v(slot)
-        return carry
-
+    def take_rest(i, carry):
+        wait_q(i)
+        place_v(i)
+        return carry
+
+    vaug_t[...] = jnp.ones((32, NODES_G), BF16)
     wait_q(0)
     prepare_q(0)
+    place_v(0)
     lax.fori_loop(0, HELD, early, 0)
-    vaug_t[...] = jnp.ones((32, NODES_G), BF16)
-    place_v(me)
-    lax.fori_loop(1, NS, take_v, 0)
+    lax.fori_loop(HELD + 1, nq, take_rest, 0)
     lax.fori_loop(0, nq - HELD, with_scores, 0)
     lax.fori_loop(nq - HELD, nq, without_scores, 0)
     o_recv[me] = o_send[me]
@@ -371,7 +380,7 @@
 
     def drain(k, carry):
         peer = lax.rem(me + k, NS)
-        for copy in (b_copy, k_copy, v_copy, q_copy, o_copy):
+        for copy in (b_copy, k_copy, qv_copy, o_copy):
             copy(peer, me).wait_send()
         return carry
 
@@ -395,9 +404,14 @@
             pltpu.VMEM((ROWS, TILES * ROWS), BF16),
             pltpu.VMEM((D, 2 * D), BF16),
             pltpu.VMEM((D, D), BF16),
-            pltpu.VMEM((D, ROWS), F32),
+            pltpu.VMEM((2 * D, ROWS), F32),
             pltpu.VMEM((NS, 1, ROWS), jnp.int32),
-        ] + [pltpu.VMEM((NS, HD, ROWS), BF16) for _ in range(8)] + [
+            pltpu.VMEM((NS, HD, ROWS), BF16),
+            pltpu.VMEM((NS, HD, ROWS), BF16),
+            pltpu.VMEM((NS, 2 * HD, ROWS), BF16),
+            pltpu.VMEM((NS, 2 * HD, ROWS), BF16),
+            pltpu.VMEM((NS, HD, ROWS), BF16),
+            pltpu.VMEM((NS, HD, ROWS), BF16),
             pltpu.VMEM((NODES_G, 128), BF16),
             pltpu.VMEM((32, NODES_G), BF16),
             pltpu.VMEM((NODES_G // QB + 1, 128, QB), BF16),
@@ -406,7 +420,7 @@
             dma((15 * CHUNKS,)),
             dma((NG, CHUNKS)),
             dma((4,)),
-        ] + [dma((NS,)) for _ in range(10)],
+        ] + [dma((NS,)) for _ in range(8)],
         compiler_params=pltpu.CompilerParams(
             collective_id=0, has_side_effects=True, vmem_limit_bytes=62 * 1024 * 1024
         ),

time: 95.5 us -> 94.6 us (level)
  no operation moved by 1% of the time
where the time goes in v4:
time: 94.6 us; the launch traced here: 94.4 us
  Pallas kernels  92.1 us (97%)
  local copies, waits for them, and re-layouts  1.62 us (2%)
    pallas_call x1, Pallas kernels, on_device(): pl.pallas_call(layer_kernel, out_shape=jax.ShapeDtypeStruct((ROWS, D), BF...  92.1 us

profile of v4, /device:TPU:1, one launch (start us, length us, event | category | flops | bytes accessed | tf_op | source)
XLA Modules:
  0.0 94.4 jit_solution(8854589526467442560)
XLA Ops:
  0.7 92.1 %layer.1 = bf16[128,768]{1,0:T(8,128)(2,1)} custom-call(bf16[128,768]{1,0:T(8,128)(2,1)} %x_ref.1, bf16[128,1024]{1,0:T(8,128)(2,1)} %tiles_ref.1, s32[1,8]{1,0:T(1,128)} %src_ref.1, s32[1]{0:T(128)S(6)} %copy.10.cnt_ref, s32[1,128]{1,0:T(1,128)} %bitcast.1, bf16[768,1536]{1,0:T(8,128)(2,1)} %wqk_ref.1, bf16[768,768]{1,0:T(8,128)(2,1)} %wv_ref.1, ...), custom_call_target="tpu_custom_call" | custom-call | tf_op jit(solution)/shard_map/layer/pallas_call | solution.py:397
  92.8 1.6 %copy.11 = bf16[128,768]{1,0:T(8,128)(2,1)} copy(bf16[128,768]{1,0:T(8,128)(2,1)} %layer.1) | data formatting | bytes 393216

commit v5 on v4

--- a/solution.py
+++ b/solution.py
@@ -158,7 +158,7 @@
         across(3, b)
         arrive(0, 1, t)
         across(1, t)
-        catch_up(2)
+        catch_up(4)
     for t, b in zip(upper, lower):
         arrive(0, 3, t)
         forward(zm, t, zp)
@@ -166,13 +166,13 @@
         forward(zp, b, zm)
         across(3, t)
         across(1, b)
-        catch_up(2)
+        catch_up(4)
     for t, b in zip(upper, lower):
         arrive(0, 2, t)
         across(2, t)
         arrive(0, 2, b)
         across(2, b)
-        catch_up(2)
+        catch_up(4)
     catch_up(0)
     own.wait()
     for load in loads:

time: 94.6 us -> 95.1 us (level)
  no operation moved by 1% of the time
where the time goes in v5:
time: 95.1 us; the launch traced here: 94.9 us
  Pallas kernels  92.6 us (97%)
  local copies, waits for them, and re-layouts  1.62 us (2%)
    pallas_call x1, Pallas kernels, on_device(): pl.pallas_call(layer_kernel, out_shape=jax.ShapeDtypeStruct((ROWS, D), BF...  92.6 us

profile of v5, /device:TPU:1, one launch (start us, length us, event | category | flops | bytes accessed | tf_op | source)
XLA Modules:
  0.0 94.9 jit_solution(8800310150628151347)
XLA Ops:
  0.7 92.6 %layer.1 = bf16[128,768]{1,0:T(8,128)(2,1)} custom-call(bf16[128,768]{1,0:T(8,128)(2,1)} %x_ref.1, bf16[128,1024]{1,0:T(8,128)(2,1)} %tiles_ref.1, s32[1,8]{1,0:T(1,128)} %src_ref.1, s32[1]{0:T(128)S(6)} %copy.10.cnt_ref, s32[1,128]{1,0:T(1,128)} %bitcast.1, bf16[768,1536]{1,0:T(8,128)(2,1)} %wqk_ref.1, bf16[768,768]{1,0:T(8,128)(2,1)} %wv_ref.1, ...), custom_call_target="tpu_custom_call" | custom-call | tf_op jit(solution)/shard_map/layer/pallas_call | solution.py:397
  93.2 1.6 %copy.11 = bf16[128,768]{1,0:T(8,128)(2,1)} copy(bf16[128,768]{1,0:T(8,128)(2,1)} %layer.1) | data formatting | bytes 393216
